TPU v7x, 256 devices: a whole 4x4x8 slice. The times are simulated.
256 devices in a mesh: segment: 8 (over x_lo, y), lat: 16 (over z, x_hi), dp: 2 (over core).
Axes of the slice: x: 4 (x_hi: 2, x_lo: 2; x = x_hi * 2 + x_lo), y: 4, z: 8, core: 2. Of those that a mesh axis runs over, the one named last changes fastest.
Arguments:
- initial: bfloat16 [8, 192, 32, 128], P('dp', None, 'lat'), may hold values from -6 to 6
- kernel: bfloat16 [8, 192, 9, 192], P('segment'), may hold values from -0.078125 to 0.078125
- bias: float32 [8, 192], P('segment'), may hold values from -0.6 to 0.6
- cotangent: bfloat16 [2, 8, 192, 32, 128], P(None, 'dp', None, 'lat'), may hold values from -6 to 6
Outputs:
- section_out: bfloat16 [8, 8, 192, 32, 128], P('segment', 'dp', None, 'lat')
- state_adjoint: float32 [8, 8, 192, 32, 128], P('segment', 'dp', None, 'lat')
- kernel_grad: float32 [8, 192, 9, 192], P('segment')
- bias_grad: float32 [8, 192], P('segment')
All inputs are finite; a program needn't handle non-finite values.
Results may differ from a plain program's by a relative error of at most 0.028.
Values may be sent and summed in bfloat16 or wider, within the bound.
A program may use at most 64 MiB of HBM per device.

v0:
```python
import math
import jax
import jax.numpy as jnp
from jax import lax
from jax.sharding import PartitionSpec as P

STEPS = 2


def passed_along(value, axis, steps):
    count = lax.axis_size(axis)
    pairs = [(source, (source + steps) % count) for source in range(count)]
    return lax.ppermute(value, axis, pairs)


def padded_2(block, sides, width):
    for axis, dim in sides:
        count = lax.axis_size(axis)
        forward = [(i, i + 1) for i in range(count - 1)]
        backward = [(target, source) for source, target in forward]
        low = lax.ppermute(
            lax.slice_in_dim(block, block.shape[dim] - width, None, axis=dim), axis, forward
        )
        high = lax.ppermute(lax.slice_in_dim(block, 0, width, axis=dim), axis, backward)
        block = jnp.concatenate([low, block, high], axis=dim)
    return block


def silu_value(values):
    return values / (1.0 + jnp.exp(-values))


def silu_slope(values):
    sigmoid_v = 1.0 / (1.0 + jnp.exp(-values))
    return sigmoid_v * (1.0 + values * (1.0 - sigmoid_v))


def tap_columns(padded):
    band_rows = padded.shape[1] - 2
    pieces = []
    for row_tap in range(3):
        strip = padded[:, row_tap : row_tap + band_rows, :]
        for col_tap in range(3):
            pieces.append(jnp.roll(strip, 1 - col_tap, axis=2))
    stacked = jnp.stack(pieces, axis=0)
    return stacked.reshape(9 * padded.shape[0], band_rows * padded.shape[2])


def back_columns(padded):
    band_rows = padded.shape[1] - 2
    pieces = []
    for row_tap in range(3):
        strip = padded[:, 2 - row_tap : 2 - row_tap + band_rows, :]
        for col_tap in range(3):
            pieces.append(jnp.roll(strip, col_tap - 1, axis=2))
    stacked = jnp.stack(pieces, axis=0)
    return stacked.reshape(9, padded.shape[0], band_rows * padded.shape[2])


def take_slot(buffer, slot):
    return lax.dynamic_index_in_dim(buffer, slot, 0, keepdims=False)


def put_slot(buffer, slot, value, flag):
    previous = lax.dynamic_index_in_dim(buffer, slot, 0, keepdims=False)
    return lax.dynamic_update_index_in_dim(buffer, jnp.where(flag, value, previous), slot, 0)


def per_device(initial, kernel, bias, cotangent):
    segment_count = lax.axis_size("segment")
    position = lax.axis_index("segment")
    before = jnp.mod(position - 1, segment_count)
    after = jnp.mod(position + 1, segment_count)
    micro = initial.shape[0]
    channels = initial.shape[1]
    band_rows = initial.shape[2]
    longitude = initial.shape[3]
    band_shape = (channels, band_rows, longitude)
    applications = STEPS * segment_count
    flat_kernel = kernel[0].reshape(channels, 9 * channels)
    kernel_taps = kernel[0]
    offsets = bias[0][:, None, None]
    cot_flat = cotangent.reshape((STEPS * micro,) + band_shape)
    tick_count = STEPS * (segment_count + micro - 1)

    def plan(moment, where_at):
        phase_span = segment_count + micro - 1
        rollout_step = jnp.floor_divide(moment, phase_span)
        sample = moment - rollout_step * phase_span - where_at
        applied = rollout_step * segment_count + where_at
        active = (moment >= 0) & (rollout_step < STEPS) & (sample >= 0) & (sample < micro)
        return (jnp.clip(sample, 0, micro - 1), applied, active)

    zero_band = jnp.zeros(band_shape, jnp.bfloat16)
    acts_store = jnp.zeros((STEPS * micro, channels, band_rows + 2, longitude), jnp.bfloat16)

    def forward_tick(moment, carry):
        outgoing, arrived, saved_states, acts_kept, last_outputs = carry
        received = passed_along(outgoing, "segment", 1)
        sent_sample, sent_applied, sent_active = plan(moment - 1, before)
        arrived = put_slot(
            arrived, sent_sample, received, sent_active & (sent_applied < applications - 1)
        )
        sample, applied, active = plan(moment, position)
        current = jnp.where(applied == 0, take_slot(initial, sample), take_slot(arrived, sample))
        activated = silu_value(current.astype(jnp.float32)).astype(jnp.bfloat16)
        padded = padded_2(activated, (("lat", 1),), 1)

        def advance(unused):
            branch = jnp.dot(
                flat_kernel, tap_columns(padded), preferred_element_type=jnp.float32
            ).reshape(band_shape)
            return (current.astype(jnp.float32) + branch + offsets).astype(jnp.bfloat16)

        def holding(unused):
            return current

        produced = lax.cond(active, advance, holding, 0)
        slot = jnp.clip(applied // segment_count, 0, STEPS - 1) * micro + sample
        saved_states = put_slot(saved_states, slot, current, active)
        acts_kept = put_slot(acts_kept, slot, padded, active)
        last_outputs = put_slot(
            last_outputs, sample, produced, active & (applied >= applications - segment_count)
        )
        return (produced, arrived, saved_states, acts_kept, last_outputs)

    forward_start = (
        zero_band,
        jnp.zeros((micro,) + band_shape, jnp.bfloat16),
        jnp.zeros((STEPS * micro,) + band_shape, jnp.bfloat16),
        acts_store,
        jnp.zeros((micro,) + band_shape, jnp.bfloat16),
    )
    unused_out, unused_arrived, saved_states, acts_kept, last_outputs = lax.fori_loop(
        0, tick_count, forward_tick, forward_start
    )

    def backward_tick(turn, carry):
        outgoing, arrived, adjoints, kernel_sum, bias_sum = carry
        received = passed_along(outgoing, "segment", -1)
        sent_sample, sent_applied, sent_active = plan(tick_count - turn, after)
        arrived = put_slot(arrived, sent_sample, received, sent_active & (sent_applied >= 1))
        sample, applied, active = plan(tick_count - 1 - turn, position)
        incoming = jnp.where(
            applied == applications - 1,
            take_slot(cot_flat, (STEPS - 1) * micro + sample),
            take_slot(arrived, sample),
        )
        incoming_padded = padded_2(incoming, (("lat", 1),), 1)
        slot = jnp.clip(applied // segment_count, 0, STEPS - 1) * micro + sample
        current = take_slot(saved_states, slot)
        padded = take_slot(acts_kept, slot)
        step_end = (applied >= segment_count) & (jnp.mod(applied, segment_count) == 0)
        cot_slot = jnp.clip(applied // segment_count - 1, 0, STEPS - 1) * micro + sample

        def retreat(unused):
            gradient_rows = incoming.reshape(channels, band_rows * longitude)
            kernel_term = lax.dot_general(
                gradient_rows,
                tap_columns(padded),
                (((1,), (1,)), ((), ())),
                preferred_element_type=jnp.float32,
            )
            bias_term = jnp.sum(incoming.astype(jnp.float32), axis=(1, 2))
            transposed = lax.dot_general(
                kernel_taps,
                back_columns(incoming_padded),
                (((0, 1), (1, 0)), ((), ())),
                preferred_element_type=jnp.float32,
            ).reshape(band_shape)
            adjoint_here = (
                incoming.astype(jnp.float32) + silu_slope(current.astype(jnp.float32)) * transposed
            )
            adjoint_here = adjoint_here + jnp.where(
                step_end, take_slot(cot_flat, cot_slot).astype(jnp.float32), 0.0
            )
            return (kernel_sum + kernel_term, bias_sum + bias_term, adjoint_here)

        def resting(unused):
            return (kernel_sum, bias_sum, jnp.zeros(band_shape, jnp.float32))

        kernel_sum, bias_sum, adjoint_here = lax.cond(active, retreat, resting, 0)
        adjoints = put_slot(adjoints, sample, adjoint_here, active & (applied < segment_count))
        return (adjoint_here.astype(jnp.bfloat16), arrived, adjoints, kernel_sum, bias_sum)

    backward_start = (
        zero_band,
        jnp.zeros((micro,) + band_shape, jnp.bfloat16),
        jnp.zeros((micro,) + band_shape, jnp.float32),
        jnp.zeros((channels, 9 * channels), jnp.float32),
        jnp.zeros((channels,), jnp.float32),
    )
    unused_grad, unused_inbox, adjoints, kernel_sum, bias_sum = lax.fori_loop(
        0, tick_count, backward_tick, backward_start
    )
    kernel_total, bias_total = (
        lax.psum(kernel_sum.astype(jnp.bfloat16), ("lat", "dp")).astype(jnp.float32),
        lax.psum(bias_sum.astype(jnp.bfloat16), ("lat", "dp")).astype(jnp.float32),
    )
    normalizer = 1.0 / math.sqrt(
        micro * lax.axis_size("dp") * band_rows * lax.axis_size("lat") * longitude
    )
    kernel_grad = (kernel_total * normalizer).reshape(1, channels, 9, channels)
    bias_grad = (bias_total * normalizer)[None]
    return (last_outputs[None], adjoints[None], kernel_grad, bias_grad)


def solution(mesh):
    return jax.shard_map(
        per_device,
        mesh=mesh,
        in_specs=(
            P("dp", None, "lat", None),
            P("segment", None, None, None),
            P("segment", None),
            P(None, "dp", None, "lat", None),
        ),
        out_specs=(
            P("segment", "dp", None, "lat", None),
            P("segment", "dp", None, "lat", None),
            P("segment", None, None, None),
            P("segment", None),
        ),
        check_vma=False,
    )
```

profile of v0, /device:TPU:2, one launch (start us, length us, event | category | flops | bytes accessed | tf_op | source)
XLA Modules:
  0.0 2029.5 jit_solution(11901487231347078123)
XLA Ops:
  13.8 500.7 %while.48 = (s32[]{:T(128)}, bf16[192,2,128]{2,1,0:T(2,128)(2,1)}, bf16[4,192,2,128]{3,1,2,0:T(8,128)(2,1)S(1)}, bf16[8,192,2,128]{3,2,1,0:T(2,128)(2,1)}, bf16[...) while((s32[]{:T(128)}, bf16[192,2,128]{2,1,0:T(2,128)(2,1)}, ...), condition=%wide.region_3.4_spmd, body=%wide.region_0.3_spmd.sunk | while | flops 172425280 | bytes 14624630 | solution.py:134
  95.0 11.4 collective-permute-done
  340.8 15.1 collective-permute-done
  517.5 1142.3 %while.49 = (s32[]{:T(128)}, bf16[192,2,128]{2,1,0:T(2,128)(2,1)}, bf16[4,192,2,128]{3,2,1,0:T(2,128)(2,1)}, f32[4,192,2,128]{3,2,1,0:T(2,128)}, f32[192,1728]{1...) while((s32[]{:T(128)}, bf16[192,2,128]{2,1,0:T(2,128)(2,1)}, ...), condition=%wide.region_8.9_spmd, body=%wide.region_4.8_spmd.sunk | while | flops 343953472 | bytes 20231204 | solution.py:193
  594.2 97.0 %collective-permute-done.3 = bf16[192,2,128]{2,1,0:T(2,128)(2,1)S(1)} collective-permute-done((bf16[192,2,128]{2,1,0:T(2,128)(2,1)}, bf16[192,2,128]{2,1,0:T(2,128)(2,1)S(1)}, u32[]{:S(2)}, u32[]{:S(2)}) %collective-permute-start.3) | collective-permute-done | bytes 98336 | tf_op jit(solution)/shard_map/while/body/eval_jaxpr/ppermute | solution.py:13
  704.0 33.2 %conditional.5 = (f32[192,1728]{1,0:T(8,128)S(1)}, f32[192]{0:T(256)S(1)}, f32[192,2,128]{2,1,0:T(2,128)}, bf16[192,2,128]{2,1,0:T(2,128)(2,1)}) conditional(s32[]{:T(128)} %convert_element_type.170, (f32[192,1728]{1,0:T(8,128)S(1)}, f32[192]{0:T(256)S(1)}) %tuple.180, (s32[]{:T(128)}, s32[]{:T(128)}, pred[]{:T(512)}, pred[]{:T(512)}, ...), branch_computations={%region_5.5_spmd, %region_6.7_spmd.clone} | conditional | flops 343216128 | bytes 17083920 | solution.py:182
  749.2 11.7 collective-permute-start.5
  765.0 33.2 %conditional.5 = (f32[192,1728]{1,0:T(8,128)S(1)}, f32[192]{0:T(256)S(1)}, f32[192,2,128]{2,1,0:T(2,128)}, bf16[192,2,128]{2,1,0:T(2,128)(2,1)}) conditional(s32[]{:T(128)} %convert_element_type.170, (f32[192,1728]{1,0:T(8,128)S(1)}, f32[192]{0:T(256)S(1)}) %tuple.180, (s32[]{:T(128)}, s32[]{:T(128)}, pred[]{:T(512)}, pred[]{:T(512)}, ...), branch_computations={%region_5.5_spmd, %region_6.7_spmd.clone} | conditional | flops 343216128 | bytes 17083920 | solution.py:182
  821.1 33.2 %conditional.5 = (f32[192,1728]{1,0:T(8,128)S(1)}, f32[192]{0:T(256)S(1)}, f32[192,2,128]{2,1,0:T(2,128)}, bf16[192,2,128]{2,1,0:T(2,128)(2,1)}) conditional(s32[]{:T(128)} %convert_element_type.170, (f32[192,1728]{1,0:T(8,128)S(1)}, f32[192]{0:T(256)S(1)}) %tuple.180, (s32[]{:T(128)}, s32[]{:T(128)}, pred[]{:T(512)}, pred[]{:T(512)}, ...), branch_computations={%region_5.5_spmd, %region_6.7_spmd.clone} | conditional | flops 343216128 | bytes 17083920 | solution.py:182
  874.7 33.2 %conditional.5 = (f32[192,1728]{1,0:T(8,128)S(1)}, f32[192]{0:T(256)S(1)}, f32[192,2,128]{2,1,0:T(2,128)}, bf16[192,2,128]{2,1,0:T(2,128)(2,1)}) conditional(s32[]{:T(128)} %convert_element_type.170, (f32[192,1728]{1,0:T(8,128)S(1)}, f32[192]{0:T(256)S(1)}) %tuple.180, (s32[]{:T(128)}, s32[]{:T(128)}, pred[]{:T(512)}, pred[]{:T(512)}, ...), branch_computations={%region_5.5_spmd, %region_6.7_spmd.clone} | conditional | flops 343216128 | bytes 17083920 | solution.py:182
  934.9 33.9 %collective-permute-start.3 = (bf16[192,2,128]{2,1,0:T(2,128)(2,1)}, bf16[192,2,128]{2,1,0:T(2,128)(2,1)S(1)}, u32[]{:S(2)}, u32[]{:S(2)}) collective-permute-start(bf16[192,2,128]{2,1,0:T(2,128)(2,1)} %get-tuple-element.1480), channel_id=1, source_target_pairs={{0,224},{32,0},{64,32},{96,64},{128,96},{160,128},{192,160},{224,1... | collective-permute-start | bytes 294920 | tf_op jit(solution)/shard_map/while/body/eval_jaxpr/ppermute | solution.py:13
  1014.9 30.2 %collective-permute-start.3 = (bf16[192,2,128]{2,1,0:T(2,128)(2,1)}, bf16[192,2,128]{2,1,0:T(2,128)(2,1)S(1)}, u32[]{:S(2)}, u32[]{:S(2)}) collective-permute-start(bf16[192,2,128]{2,1,0:T(2,128)(2,1)} %get-tuple-element.1480), channel_id=1, source_target_pairs={{0,224},{32,0},{64,32},{96,64},{128,96},{160,128},{192,160},{224,1... | collective-permute-start | bytes 294920 | tf_op jit(solution)/shard_map/while/body/eval_jaxpr/ppermute | solution.py:13
  1087.3 29.7 %collective-permute-start.3 = (bf16[192,2,128]{2,1,0:T(2,128)(2,1)}, bf16[192,2,128]{2,1,0:T(2,128)(2,1)S(1)}, u32[]{:S(2)}, u32[]{:S(2)}) collective-permute-start(bf16[192,2,128]{2,1,0:T(2,128)(2,1)} %get-tuple-element.1480), channel_id=1, source_target_pairs={{0,224},{32,0},{64,32},{96,64},{128,96},{160,128},{192,160},{224,1... | collective-permute-start | bytes 294920 | tf_op jit(solution)/shard_map/while/body/eval_jaxpr/ppermute | solution.py:13
  1145.6 13.3 collective-permute-start.5
  1164.7 30.2 %collective-permute-start.3 = (bf16[192,2,128]{2,1,0:T(2,128)(2,1)}, bf16[192,2,128]{2,1,0:T(2,128)(2,1)S(1)}, u32[]{:S(2)}, u32[]{:S(2)}) collective-permute-start(bf16[192,2,128]{2,1,0:T(2,128)(2,1)} %get-tuple-element.1480), channel_id=1, source_target_pairs={{0,224},{32,0},{64,32},{96,64},{128,96},{160,128},{192,160},{224,1... | collective-permute-start | bytes 294920 | tf_op jit(solution)/shard_map/while/body/eval_jaxpr/ppermute | solution.py:13
  1195.8 94.5 %collective-permute-done.3 = bf16[192,2,128]{2,1,0:T(2,128)(2,1)S(1)} collective-permute-done((bf16[192,2,128]{2,1,0:T(2,128)(2,1)}, bf16[192,2,128]{2,1,0:T(2,128)(2,1)S(1)}, u32[]{:S(2)}, u32[]{:S(2)}) %collective-permute-start.3) | collective-permute-done | bytes 98336 | tf_op jit(solution)/shard_map/while/body/eval_jaxpr/ppermute | solution.py:13
  1305.7 33.2 %conditional.5 = (f32[192,1728]{1,0:T(8,128)S(1)}, f32[192]{0:T(256)S(1)}, f32[192,2,128]{2,1,0:T(2,128)}, bf16[192,2,128]{2,1,0:T(2,128)(2,1)}) conditional(s32[]{:T(128)} %convert_element_type.170, (f32[192,1728]{1,0:T(8,128)S(1)}, f32[192]{0:T(256)S(1)}) %tuple.180, (s32[]{:T(128)}, s32[]{:T(128)}, pred[]{:T(512)}, pred[]{:T(512)}, ...), branch_computations={%region_5.5_spmd, %region_6.7_spmd.clone} | conditional | flops 343216128 | bytes 17083920 | solution.py:182
  1360.4 33.2 %conditional.5 = (f32[192,1728]{1,0:T(8,128)S(1)}, f32[192]{0:T(256)S(1)}, f32[192,2,128]{2,1,0:T(2,128)}, bf16[192,2,128]{2,1,0:T(2,128)(2,1)}) conditional(s32[]{:T(128)} %convert_element_type.170, (f32[192,1728]{1,0:T(8,128)S(1)}, f32[192]{0:T(256)S(1)}) %tuple.180, (s32[]{:T(128)}, s32[]{:T(128)}, pred[]{:T(512)}, pred[]{:T(512)}, ...), branch_computations={%region_5.5_spmd, %region_6.7_spmd.clone} | conditional | flops 343216128 | bytes 17083920 | solution.py:182
  1417.6 33.2 %conditional.5 = (f32[192,1728]{1,0:T(8,128)S(1)}, f32[192]{0:T(256)S(1)}, f32[192,2,128]{2,1,0:T(2,128)}, bf16[192,2,128]{2,1,0:T(2,128)(2,1)}) conditional(s32[]{:T(128)} %convert_element_type.170, (f32[192,1728]{1,0:T(8,128)S(1)}, f32[192]{0:T(256)S(1)}) %tuple.180, (s32[]{:T(128)}, s32[]{:T(128)}, pred[]{:T(512)}, pred[]{:T(512)}, ...), branch_computations={%region_5.5_spmd, %region_6.7_spmd.clone} | conditional | flops 343216128 | bytes 17083920 | solution.py:182
  1472.3 33.2 %conditional.5 = (f32[192,1728]{1,0:T(8,128)S(1)}, f32[192]{0:T(256)S(1)}, f32[192,2,128]{2,1,0:T(2,128)}, bf16[192,2,128]{2,1,0:T(2,128)(2,1)}) conditional(s32[]{:T(128)} %convert_element_type.170, (f32[192,1728]{1,0:T(8,128)S(1)}, f32[192]{0:T(256)S(1)}) %tuple.180, (s32[]{:T(128)}, s32[]{:T(128)}, pred[]{:T(512)}, pred[]{:T(512)}, ...), branch_computations={%region_5.5_spmd, %region_6.7_spmd.clone} | conditional | flops 343216128 | bytes 17083920 | solution.py:182
  1530.8 37.3 %collective-permute-start.3 = (bf16[192,2,128]{2,1,0:T(2,128)(2,1)}, bf16[192,2,128]{2,1,0:T(2,128)(2,1)S(1)}, u32[]{:S(2)}, u32[]{:S(2)}) collective-permute-start(bf16[192,2,128]{2,1,0:T(2,128)(2,1)} %get-tuple-element.1480), channel_id=1, source_target_pairs={{0,224},{32,0},{64,32},{96,64},{128,96},{160,128},{192,160},{224,1... | collective-permute-start | bytes 294920 | tf_op jit(solution)/shard_map/while/body/eval_jaxpr/ppermute | solution.py:13
  1612.2 29.8 %collective-permute-start.3 = (bf16[192,2,128]{2,1,0:T(2,128)(2,1)}, bf16[192,2,128]{2,1,0:T(2,128)(2,1)S(1)}, u32[]{:S(2)}, u32[]{:S(2)}) collective-permute-start(bf16[192,2,128]{2,1,0:T(2,128)(2,1)} %get-tuple-element.1480), channel_id=1, source_target_pairs={{0,224},{32,0},{64,32},{96,64},{128,96},{160,128},{192,160},{224,1... | collective-permute-start | bytes 294920 | tf_op jit(solution)/shard_map/while/body/eval_jaxpr/ppermute | solution.py:13
  1660.8 94.2 %psum.15 = bf16[192]{0:T(256)(128)(2,1)S(1)} all-reduce(bf16[192]{0:T(256)(128)(2,1)S(1)} %convert_element_type.117), channel_id=1, replica_groups=mesh['segment'=8,'lat'=16,'dp'=2] {'lat','dp'}, use_global_device_ids=true, to_apply=%region_10.11 | all-reduce | flops 192 | bytes 768 | tf_op jit(solution)/shard_map/psum | solution.py:198
  1755.5 261.1 %all-reduce.2.cloned.1.call-done = bf16[192,1728]{1,0:T(8,128)(2,1)} async-done(((bf16[192,1728]{1,0:T(8,128)(2,1)}), bf16[192,1728]{1,0:T(8,128)(2,1)}) %all-reduce.2.cloned.1.call-update) | async-done | bytes 663568 | tf_op jit(solution)/shard_map/psum | solution.py:197
  (1382 shorter events, 1287.8 us)
Async XLA Ops:
  7.2 2009.5 %all-reduce.2.cloned.1.call-start = ((), (), s32[]{:S(2)}) async-start(), calls=%async_computation | async-start | bytes 1376256 | tf_op jit(solution)/shard_map/psum | solution.py:197
  92.5 13.8 collective-permute-start
  338.4 17.6 collective-permute-start
  526.7 12.5 collective-permute-start.5
  572.1 12.3 collective-permute-start.4
  573.4 12.0 collective-permute-start.5
  588.9 102.3 %collective-permute-start.3 = (bf16[192,2,128]{2,1,0:T(2,128)(2,1)}, bf16[192,2,128]{2,1,0:T(2,128)(2,1)S(1)}, u32[]{:S(2)}, u32[]{:S(2)}) collective-permute-start(bf16[192,2,128]{2,1,0:T(2,128)(2,1)} %get-tuple-element.1480), channel_id=1, source_target_pairs={{0,224},{32,0},{64,32},{96,64},{128,96},{160,128},{192,160},{224,1... | collective-permute-start | bytes 294920 | tf_op jit(solution)/shard_map/while/body/eval_jaxpr/ppermute | solution.py:13
  747.9 14.6 collective-permute-start.4
  749.2 15.5 collective-permute-start.5
  919.8 11.6 collective-permute-start.5
  934.9 36.4 %collective-permute-start.3 = (bf16[192,2,128]{2,1,0:T(2,128)(2,1)}, bf16[192,2,128]{2,1,0:T(2,128)(2,1)S(1)}, u32[]{:S(2)}, u32[]{:S(2)}) collective-permute-start(bf16[192,2,128]{2,1,0:T(2,128)(2,1)} %get-tuple-element.1480), channel_id=1, source_target_pairs={{0,224},{32,0},{64,32},{96,64},{128,96},{160,128},{192,160},{224,1... | collective-permute-start | bytes 294920 | tf_op jit(solution)/shard_map/while/body/eval_jaxpr/ppermute | solution.py:13
  973.2 12.1 collective-permute-start.4
  1014.9 32.7 %collective-permute-start.3 = (bf16[192,2,128]{2,1,0:T(2,128)(2,1)}, bf16[192,2,128]{2,1,0:T(2,128)(2,1)S(1)}, u32[]{:S(2)}, u32[]{:S(2)}) collective-permute-start(bf16[192,2,128]{2,1,0:T(2,128)(2,1)} %get-tuple-element.1480), channel_id=1, source_target_pairs={{0,224},{32,0},{64,32},{96,64},{128,96},{160,128},{192,160},{224,1... | collective-permute-start | bytes 294920 | tf_op jit(solution)/shard_map/while/body/eval_jaxpr/ppermute | solution.py:13
  1087.3 32.2 %collective-permute-start.3 = (bf16[192,2,128]{2,1,0:T(2,128)(2,1)}, bf16[192,2,128]{2,1,0:T(2,128)(2,1)S(1)}, u32[]{:S(2)}, u32[]{:S(2)}) collective-permute-start(bf16[192,2,128]{2,1,0:T(2,128)(2,1)} %get-tuple-element.1480), channel_id=1, source_target_pairs={{0,224},{32,0},{64,32},{96,64},{128,96},{160,128},{192,160},{224,1... | collective-permute-start | bytes 294920 | tf_op jit(solution)/shard_map/while/body/eval_jaxpr/ppermute | solution.py:13
  1144.3 16.3 collective-permute-start.4
  1145.6 15.5 collective-permute-start.5
  1164.7 125.7 %collective-permute-start.3 = (bf16[192,2,128]{2,1,0:T(2,128)(2,1)}, bf16[192,2,128]{2,1,0:T(2,128)(2,1)S(1)}, u32[]{:S(2)}, u32[]{:S(2)}) collective-permute-start(bf16[192,2,128]{2,1,0:T(2,128)(2,1)} %get-tuple-element.1480), channel_id=1, source_target_pairs={{0,224},{32,0},{64,32},{96,64},{128,96},{160,128},{192,160},{224,1... | collective-permute-start | bytes 294920 | tf_op jit(solution)/shard_map/while/body/eval_jaxpr/ppermute | solution.py:13
  1292.3 12.1 collective-permute-start.4
  1293.6 11.7 collective-permute-start.5
  1404.3 12.0 collective-permute-start.4
  1514.1 12.6 collective-permute-start.4
  1515.4 11.8 collective-permute-start.5
  1530.8 39.8 %collective-permute-start.3 = (bf16[192,2,128]{2,1,0:T(2,128)(2,1)}, bf16[192,2,128]{2,1,0:T(2,128)(2,1)S(1)}, u32[]{:S(2)}, u32[]{:S(2)}) collective-permute-start(bf16[192,2,128]{2,1,0:T(2,128)(2,1)} %get-tuple-element.1480), channel_id=1, source_target_pairs={{0,224},{32,0},{64,32},{96,64},{128,96},{160,128},{192,160},{224,1... | collective-permute-start | bytes 294920 | tf_op jit(solution)/shard_map/while/body/eval_jaxpr/ppermute | solution.py:13
  1612.2 32.3 %collective-permute-start.3 = (bf16[192,2,128]{2,1,0:T(2,128)(2,1)}, bf16[192,2,128]{2,1,0:T(2,128)(2,1)S(1)}, u32[]{:S(2)}, u32[]{:S(2)}) collective-permute-start(bf16[192,2,128]{2,1,0:T(2,128)(2,1)} %get-tuple-element.1480), channel_id=1, source_target_pairs={{0,224},{32,0},{64,32},{96,64},{128,96},{160,128},{192,160},{224,1... | collective-permute-start | bytes 294920 | tf_op jit(solution)/shard_map/while/body/eval_jaxpr/ppermute | solution.py:13
  (135 other events, 1180.8 us)
Sparse Core Ops, SparseCore 0:
  1660.9 355.7 all-reduce.1
where the time goes:
time: 2040 us; the launch traced here: 2030 us
  waiting for transfers between devices  671 us (33%)
  starting transfers between devices  631 us (31%)
  local copies, waits for them, and re-layouts  373 us (18%)
  other arithmetic  222 us (11%)
  blocking collectives  94.2 us (5%)
    ppermute x44, waiting for transfers between devices, passed_along(): return lax.ppermute(value, axis, pairs)  362 us
    ppermute x44, starting transfers between devices, padded_2(): lax.ppermute(lax.slice_in_dim(block, block.shape[dim] - width, None, axis...  334 us
    psum x1, waiting for transfers between devices, per_device(): lax.psum(kernel_sum.astype(jnp.bfloat16), ('lat', 'dp')).astype(jnp.float32)  261 us
    ppermute x44, starting transfers between devices, passed_along(): return lax.ppermute(value, axis, pairs)  240 us
    dynamic_slice x132, local copies, waits for them, and re-layouts, put_slot(): previous = lax.dynamic_index_in_dim(buffer, slot, 0, keepdims=False)  105 us
    psum x1, blocking collectives, per_device(): lax.psum(bias_sum.astype(jnp.bfloat16), ('lat', 'dp')).astype(jnp.float32)  94.2 us
    another operation x80, local copies, waits for them, and re-layouts, back_columns(): stacked = jnp.stack(pieces, axis=0)  68.2 us
    concatenate x48, other arithmetic, back_columns(): pieces.append(jnp.roll(strip, col_tap - 1, axis=2))  63.6 us
  transfers between devices with their start and end apart: 133, of which 89 were waited for; matrix products, arithmetic and copies ran while one was open for 6% of the time, Pallas kernels for 0%

commit v1 on v0

--- a/solution.py
+++ b/solution.py
@@ -194,7 +194,7 @@
         0, tick_count, backward_tick, backward_start
     )
     kernel_total, bias_total = (
-        lax.psum(kernel_sum.astype(jnp.bfloat16), ("lat", "dp")).astype(jnp.float32),
+        lax.psum(lax.psum(kernel_sum.astype(jnp.bfloat16), "lat"), "dp").astype(jnp.float32),
         lax.psum(bias_sum.astype(jnp.bfloat16), ("lat", "dp")).astype(jnp.float32),
     )
     normalizer = 1.0 / math.sqrt(

time: 2040 us -> 2000 us (0.980)
  blocking collectives: 94.2 us -> 65.1 us
    psum x1, blocking collectives: 94.2 us -> 65.1 us  [per_device(): lax.psum(bias_sum.astype(jnp.bfloat16), ('lat', 'dp')).astype(jnp.float32)]
    psum x1 -> x2, waiting for transfers between devices: 261 us -> 249 us  [the longest x1 249 us: per_device(): lax.psum(kernel_sum.astype(jnp.bfloat16), 'lat')]
  transfers between devices with their start and end apart: 133 -> 134, of which waited for: 89 -> 89; matrix products, arithmetic and copies ran while one was open for 6% -> 6% of each run, Pallas kernels for 0% -> 0%
where the time goes in v1:
time: 2000 us; the launch traced here: 1990 us
  waiting for transfers between devices  658 us (33%)
  starting transfers between devices  632 us (32%)
  local copies, waits for them, and re-layouts  357 us (18%)
  other arithmetic  236 us (12%)
  blocking collectives  65.1 us (3%)
    ppermute x44, waiting for transfers between devices, passed_along(): return lax.ppermute(value, axis, pairs)  363 us
    ppermute x44, starting transfers between devices, padded_2(): lax.ppermute(lax.slice_in_dim(block, block.shape[dim] - width, None, axis...  335 us
    psum x1, waiting for transfers between devices, per_device(): lax.psum(kernel_sum.astype(jnp.bfloat16), 'lat')  249 us
    ppermute x44, starting transfers between devices, passed_along(): return lax.ppermute(value, axis, pairs)  240 us
    dynamic_slice x132, local copies, waits for them, and re-layouts, put_slot(): previous = lax.dynamic_index_in_dim(buffer, slot, 0, keepdims=False)  104 us
    dynamic_update_slice x88, other arithmetic, put_slot(): lax.dynamic_update_index_in_dim(buffer, jnp.where(flag, value, previous),...  75.2 us
    another operation x80, local copies, waits for them, and re-layouts, back_columns(): stacked = jnp.stack(pieces, axis=0)  68.2 us
    psum x1, blocking collectives, per_device(): lax.psum(bias_sum.astype(jnp.bfloat16), ('lat', 'dp')).astype(jnp.float32)  65.1 us
  transfers between devices with their start and end apart: 134, of which 89 were waited for; matrix products, arithmetic and copies ran while one was open for 6% of the time, Pallas kernels for 0%

profile of v1, /device:TPU:2, one launch (start us, length us, event | category | flops | bytes accessed | tf_op | source)
XLA Modules:
  0.0 1986.8 jit_solution(3768999433222049584)
XLA Ops:
  13.4 499.9 %while.48 = (s32[]{:T(128)}, bf16[192,2,128]{2,1,0:T(2,128)(2,1)}, bf16[4,192,2,128]{3,1,2,0:T(8,128)(2,1)S(1)}, bf16[8,192,2,128]{3,2,1,0:T(2,128)(2,1)}, bf16[...) while((s32[]{:T(128)}, bf16[192,2,128]{2,1,0:T(2,128)(2,1)}, ...), condition=%wide.region_3.4_spmd, body=%wide.region_0.3_spmd.sunk | while | flops 172425280 | bytes 14624630 | solution.py:134
  94.3 11.4 collective-permute-done
  340.3 14.6 collective-permute-done
  516.3 1142.4 %while.49 = (s32[]{:T(128)}, bf16[192,2,128]{2,1,0:T(2,128)(2,1)}, bf16[4,192,2,128]{3,2,1,0:T(2,128)(2,1)}, f32[4,192,2,128]{3,2,1,0:T(2,128)}, f32[192,1728]{1...) while((s32[]{:T(128)}, bf16[192,2,128]{2,1,0:T(2,128)(2,1)}, ...), condition=%wide.region_8.9_spmd, body=%wide.region_4.8_spmd.sunk | while | flops 343953472 | bytes 20231204 | solution.py:193
  592.5 97.7 %collective-permute-done.3 = bf16[192,2,128]{2,1,0:T(2,128)(2,1)S(1)} collective-permute-done((bf16[192,2,128]{2,1,0:T(2,128)(2,1)}, bf16[192,2,128]{2,1,0:T(2,128)(2,1)S(1)}, u32[]{:S(2)}, u32[]{:S(2)}) %collective-permute-start.3) | collective-permute-done | bytes 98336 | tf_op jit(solution)/shard_map/while/body/eval_jaxpr/ppermute | solution.py:13
  702.9 33.2 %conditional.5 = (f32[192,1728]{1,0:T(8,128)S(1)}, f32[192]{0:T(256)S(1)}, f32[192,2,128]{2,1,0:T(2,128)}, bf16[192,2,128]{2,1,0:T(2,128)(2,1)}) conditional(s32[]{:T(128)} %convert_element_type.170, (f32[192,1728]{1,0:T(8,128)S(1)}, f32[192]{0:T(256)S(1)}) %tuple.180, (s32[]{:T(128)}, s32[]{:T(128)}, pred[]{:T(512)}, pred[]{:T(512)}, ...), branch_computations={%region_5.5_spmd, %region_6.7_spmd.clone} | conditional | flops 343216128 | bytes 17083920 | solution.py:182
  748.0 11.8 collective-permute-start.5
  763.9 33.2 %conditional.5 = (f32[192,1728]{1,0:T(8,128)S(1)}, f32[192]{0:T(256)S(1)}, f32[192,2,128]{2,1,0:T(2,128)}, bf16[192,2,128]{2,1,0:T(2,128)(2,1)}) conditional(s32[]{:T(128)} %convert_element_type.170, (f32[192,1728]{1,0:T(8,128)S(1)}, f32[192]{0:T(256)S(1)}) %tuple.180, (s32[]{:T(128)}, s32[]{:T(128)}, pred[]{:T(512)}, pred[]{:T(512)}, ...), branch_computations={%region_5.5_spmd, %region_6.7_spmd.clone} | conditional | flops 343216128 | bytes 17083920 | solution.py:182
  820.2 33.2 %conditional.5 = (f32[192,1728]{1,0:T(8,128)S(1)}, f32[192]{0:T(256)S(1)}, f32[192,2,128]{2,1,0:T(2,128)}, bf16[192,2,128]{2,1,0:T(2,128)(2,1)}) conditional(s32[]{:T(128)} %convert_element_type.170, (f32[192,1728]{1,0:T(8,128)S(1)}, f32[192]{0:T(256)S(1)}) %tuple.180, (s32[]{:T(128)}, s32[]{:T(128)}, pred[]{:T(512)}, pred[]{:T(512)}, ...), branch_computations={%region_5.5_spmd, %region_6.7_spmd.clone} | conditional | flops 343216128 | bytes 17083920 | solution.py:182
  873.7 33.2 %conditional.5 = (f32[192,1728]{1,0:T(8,128)S(1)}, f32[192]{0:T(256)S(1)}, f32[192,2,128]{2,1,0:T(2,128)}, bf16[192,2,128]{2,1,0:T(2,128)(2,1)}) conditional(s32[]{:T(128)} %convert_element_type.170, (f32[192,1728]{1,0:T(8,128)S(1)}, f32[192]{0:T(256)S(1)}) %tuple.180, (s32[]{:T(128)}, s32[]{:T(128)}, pred[]{:T(512)}, pred[]{:T(512)}, ...), branch_computations={%region_5.5_spmd, %region_6.7_spmd.clone} | conditional | flops 343216128 | bytes 17083920 | solution.py:182
  933.9 33.9 %collective-permute-start.3 = (bf16[192,2,128]{2,1,0:T(2,128)(2,1)}, bf16[192,2,128]{2,1,0:T(2,128)(2,1)S(1)}, u32[]{:S(2)}, u32[]{:S(2)}) collective-permute-start(bf16[192,2,128]{2,1,0:T(2,128)(2,1)} %get-tuple-element.1480), channel_id=1, source_target_pairs={{0,224},{32,0},{64,32},{96,64},{128,96},{160,128},{192,160},{224,1... | collective-permute-start | bytes 294920 | tf_op jit(solution)/shard_map/while/body/eval_jaxpr/ppermute | solution.py:13
  1013.8 30.2 %collective-permute-start.3 = (bf16[192,2,128]{2,1,0:T(2,128)(2,1)}, bf16[192,2,128]{2,1,0:T(2,128)(2,1)S(1)}, u32[]{:S(2)}, u32[]{:S(2)}) collective-permute-start(bf16[192,2,128]{2,1,0:T(2,128)(2,1)} %get-tuple-element.1480), channel_id=1, source_target_pairs={{0,224},{32,0},{64,32},{96,64},{128,96},{160,128},{192,160},{224,1... | collective-permute-start | bytes 294920 | tf_op jit(solution)/shard_map/while/body/eval_jaxpr/ppermute | solution.py:13
  1086.3 29.7 %collective-permute-start.3 = (bf16[192,2,128]{2,1,0:T(2,128)(2,1)}, bf16[192,2,128]{2,1,0:T(2,128)(2,1)S(1)}, u32[]{:S(2)}, u32[]{:S(2)}) collective-permute-start(bf16[192,2,128]{2,1,0:T(2,128)(2,1)} %get-tuple-element.1480), channel_id=1, source_target_pairs={{0,224},{32,0},{64,32},{96,64},{128,96},{160,128},{192,160},{224,1... | collective-permute-start | bytes 294920 | tf_op jit(solution)/shard_map/while/body/eval_jaxpr/ppermute | solution.py:13
  1144.6 13.3 collective-permute-start.5
  1163.6 30.2 %collective-permute-start.3 = (bf16[192,2,128]{2,1,0:T(2,128)(2,1)}, bf16[192,2,128]{2,1,0:T(2,128)(2,1)S(1)}, u32[]{:S(2)}, u32[]{:S(2)}) collective-permute-start(bf16[192,2,128]{2,1,0:T(2,128)(2,1)} %get-tuple-element.1480), channel_id=1, source_target_pairs={{0,224},{32,0},{64,32},{96,64},{128,96},{160,128},{192,160},{224,1... | collective-permute-start | bytes 294920 | tf_op jit(solution)/shard_map/while/body/eval_jaxpr/ppermute | solution.py:13
  1194.7 94.5 %collective-permute-done.3 = bf16[192,2,128]{2,1,0:T(2,128)(2,1)S(1)} collective-permute-done((bf16[192,2,128]{2,1,0:T(2,128)(2,1)}, bf16[192,2,128]{2,1,0:T(2,128)(2,1)S(1)}, u32[]{:S(2)}, u32[]{:S(2)}) %collective-permute-start.3) | collective-permute-done | bytes 98336 | tf_op jit(solution)/shard_map/while/body/eval_jaxpr/ppermute | solution.py:13
  1304.5 33.2 %conditional.5 = (f32[192,1728]{1,0:T(8,128)S(1)}, f32[192]{0:T(256)S(1)}, f32[192,2,128]{2,1,0:T(2,128)}, bf16[192,2,128]{2,1,0:T(2,128)(2,1)}) conditional(s32[]{:T(128)} %convert_element_type.170, (f32[192,1728]{1,0:T(8,128)S(1)}, f32[192]{0:T(256)S(1)}) %tuple.180, (s32[]{:T(128)}, s32[]{:T(128)}, pred[]{:T(512)}, pred[]{:T(512)}, ...), branch_computations={%region_5.5_spmd, %region_6.7_spmd.clone} | conditional | flops 343216128 | bytes 17083920 | solution.py:182
  1359.3 33.2 %conditional.5 = (f32[192,1728]{1,0:T(8,128)S(1)}, f32[192]{0:T(256)S(1)}, f32[192,2,128]{2,1,0:T(2,128)}, bf16[192,2,128]{2,1,0:T(2,128)(2,1)}) conditional(s32[]{:T(128)} %convert_element_type.170, (f32[192,1728]{1,0:T(8,128)S(1)}, f32[192]{0:T(256)S(1)}) %tuple.180, (s32[]{:T(128)}, s32[]{:T(128)}, pred[]{:T(512)}, pred[]{:T(512)}, ...), branch_computations={%region_5.5_spmd, %region_6.7_spmd.clone} | conditional | flops 343216128 | bytes 17083920 | solution.py:182
  1416.5 33.2 %conditional.5 = (f32[192,1728]{1,0:T(8,128)S(1)}, f32[192]{0:T(256)S(1)}, f32[192,2,128]{2,1,0:T(2,128)}, bf16[192,2,128]{2,1,0:T(2,128)(2,1)}) conditional(s32[]{:T(128)} %convert_element_type.170, (f32[192,1728]{1,0:T(8,128)S(1)}, f32[192]{0:T(256)S(1)}) %tuple.180, (s32[]{:T(128)}, s32[]{:T(128)}, pred[]{:T(512)}, pred[]{:T(512)}, ...), branch_computations={%region_5.5_spmd, %region_6.7_spmd.clone} | conditional | flops 343216128 | bytes 17083920 | solution.py:182
  1471.2 33.2 %conditional.5 = (f32[192,1728]{1,0:T(8,128)S(1)}, f32[192]{0:T(256)S(1)}, f32[192,2,128]{2,1,0:T(2,128)}, bf16[192,2,128]{2,1,0:T(2,128)(2,1)}) conditional(s32[]{:T(128)} %convert_element_type.170, (f32[192,1728]{1,0:T(8,128)S(1)}, f32[192]{0:T(256)S(1)}) %tuple.180, (s32[]{:T(128)}, s32[]{:T(128)}, pred[]{:T(512)}, pred[]{:T(512)}, ...), branch_computations={%region_5.5_spmd, %region_6.7_spmd.clone} | conditional | flops 343216128 | bytes 17083920 | solution.py:182
  1529.7 37.3 %collective-permute-start.3 = (bf16[192,2,128]{2,1,0:T(2,128)(2,1)}, bf16[192,2,128]{2,1,0:T(2,128)(2,1)S(1)}, u32[]{:S(2)}, u32[]{:S(2)}) collective-permute-start(bf16[192,2,128]{2,1,0:T(2,128)(2,1)} %get-tuple-element.1480), channel_id=1, source_target_pairs={{0,224},{32,0},{64,32},{96,64},{128,96},{160,128},{192,160},{224,1... | collective-permute-start | bytes 294920 | tf_op jit(solution)/shard_map/while/body/eval_jaxpr/ppermute | solution.py:13
  1611.1 29.8 %collective-permute-start.3 = (bf16[192,2,128]{2,1,0:T(2,128)(2,1)}, bf16[192,2,128]{2,1,0:T(2,128)(2,1)S(1)}, u32[]{:S(2)}, u32[]{:S(2)}) collective-permute-start(bf16[192,2,128]{2,1,0:T(2,128)(2,1)} %get-tuple-element.1480), channel_id=1, source_target_pairs={{0,224},{32,0},{64,32},{96,64},{128,96},{160,128},{192,160},{224,1... | collective-permute-start | bytes 294920 | tf_op jit(solution)/shard_map/while/body/eval_jaxpr/ppermute | solution.py:13
  1659.7 248.5 %all-reduce.3.cloned.1.call-done = bf16[192,1728]{1,0:T(8,128)(2,1)} async-done(((bf16[192,1728]{1,0:T(8,128)(2,1)}), bf16[192,1728]{1,0:T(8,128)(2,1)}) %all-reduce.3.cloned.1.call-update) | async-done | bytes 663568 | tf_op jit(solution)/shard_map/psum | solution.py:197
  1908.3 65.1 %psum.23 = bf16[192]{0:T(256)(128)(2,1)S(1)} all-reduce(bf16[192]{0:T(256)(128)(2,1)S(1)} %convert_element_type.117), channel_id=1, replica_groups=mesh['segment'=8,'lat'=16,'dp'=2] {'lat','dp'}, use_global_device_ids=true, to_apply=%region_11.12 | all-reduce | flops 192 | bytes 768 | tf_op jit(solution)/shard_map/psum | solution.py:198
  (1385 shorter events, 1286.6 us)
Async XLA Ops:
  7.2 1901.1 %all-reduce.3.cloned.1.call-start = ((), (), s32[]{:S(2)}) async-start(), calls=%async_computation | async-start | bytes 1376256 | tf_op jit(solution)/shard_map/psum | solution.py:197
  91.9 13.8 collective-permute-start
  337.9 17.0 collective-permute-start
  524.2 11.5 collective-permute-start.4
  587.8 102.3 %collective-permute-start.3 = (bf16[192,2,128]{2,1,0:T(2,128)(2,1)}, bf16[192,2,128]{2,1,0:T(2,128)(2,1)S(1)}, u32[]{:S(2)}, u32[]{:S(2)}) collective-permute-start(bf16[192,2,128]{2,1,0:T(2,128)(2,1)} %get-tuple-element.1480), channel_id=1, source_target_pairs={{0,224},{32,0},{64,32},{96,64},{128,96},{160,128},{192,160},{224,1... | collective-permute-start | bytes 294920 | tf_op jit(solution)/shard_map/while/body/eval_jaxpr/ppermute | solution.py:13
  746.7 14.8 collective-permute-start.4
  748.0 15.5 collective-permute-start.5
  918.8 11.6 collective-permute-start.5
  933.9 36.4 %collective-permute-start.3 = (bf16[192,2,128]{2,1,0:T(2,128)(2,1)}, bf16[192,2,128]{2,1,0:T(2,128)(2,1)S(1)}, u32[]{:S(2)}, u32[]{:S(2)}) collective-permute-start(bf16[192,2,128]{2,1,0:T(2,128)(2,1)} %get-tuple-element.1480), channel_id=1, source_target_pairs={{0,224},{32,0},{64,32},{96,64},{128,96},{160,128},{192,160},{224,1... | collective-permute-start | bytes 294920 | tf_op jit(solution)/shard_map/while/body/eval_jaxpr/ppermute | solution.py:13
  972.2 12.1 collective-permute-start.4
  1013.8 32.7 %collective-permute-start.3 = (bf16[192,2,128]{2,1,0:T(2,128)(2,1)}, bf16[192,2,128]{2,1,0:T(2,128)(2,1)S(1)}, u32[]{:S(2)}, u32[]{:S(2)}) collective-permute-start(bf16[192,2,128]{2,1,0:T(2,128)(2,1)} %get-tuple-element.1480), channel_id=1, source_target_pairs={{0,224},{32,0},{64,32},{96,64},{128,96},{160,128},{192,160},{224,1... | collective-permute-start | bytes 294920 | tf_op jit(solution)/shard_map/while/body/eval_jaxpr/ppermute | solution.py:13
  1086.3 32.2 %collective-permute-start.3 = (bf16[192,2,128]{2,1,0:T(2,128)(2,1)}, bf16[192,2,128]{2,1,0:T(2,128)(2,1)S(1)}, u32[]{:S(2)}, u32[]{:S(2)}) collective-permute-start(bf16[192,2,128]{2,1,0:T(2,128)(2,1)} %get-tuple-element.1480), channel_id=1, source_target_pairs={{0,224},{32,0},{64,32},{96,64},{128,96},{160,128},{192,160},{224,1... | collective-permute-start | bytes 294920 | tf_op jit(solution)/shard_map/while/body/eval_jaxpr/ppermute | solution.py:13
  1143.3 16.2 collective-permute-start.4
  1144.6 15.5 collective-permute-start.5
  1163.6 125.7 %collective-permute-start.3 = (bf16[192,2,128]{2,1,0:T(2,128)(2,1)}, bf16[192,2,128]{2,1,0:T(2,128)(2,1)S(1)}, u32[]{:S(2)}, u32[]{:S(2)}) collective-permute-start(bf16[192,2,128]{2,1,0:T(2,128)(2,1)} %get-tuple-element.1480), channel_id=1, source_target_pairs={{0,224},{32,0},{64,32},{96,64},{128,96},{160,128},{192,160},{224,1... | collective-permute-start | bytes 294920 | tf_op jit(solution)/shard_map/while/body/eval_jaxpr/ppermute | solution.py:13
  1291.2 12.1 collective-permute-start.4
  1292.5 11.7 collective-permute-start.5
  1403.2 12.0 collective-permute-start.4
  1404.5 11.6 collective-permute-start.5
  1513.0 12.6 collective-permute-start.4
  1514.3 11.9 collective-permute-start.5
  1529.7 39.8 %collective-permute-start.3 = (bf16[192,2,128]{2,1,0:T(2,128)(2,1)}, bf16[192,2,128]{2,1,0:T(2,128)(2,1)S(1)}, u32[]{:S(2)}, u32[]{:S(2)}) collective-permute-start(bf16[192,2,128]{2,1,0:T(2,128)(2,1)} %get-tuple-element.1480), channel_id=1, source_target_pairs={{0,224},{32,0},{64,32},{96,64},{128,96},{160,128},{192,160},{224,1... | collective-permute-start | bytes 294920 | tf_op jit(solution)/shard_map/while/body/eval_jaxpr/ppermute | solution.py:13
  1611.1 32.3 %collective-permute-start.3 = (bf16[192,2,128]{2,1,0:T(2,128)(2,1)}, bf16[192,2,128]{2,1,0:T(2,128)(2,1)S(1)}, u32[]{:S(2)}, u32[]{:S(2)}) collective-permute-start(bf16[192,2,128]{2,1,0:T(2,128)(2,1)} %get-tuple-element.1480), channel_id=1, source_target_pairs={{0,224},{32,0},{64,32},{96,64},{128,96},{160,128},{192,160},{224,1... | collective-permute-start | bytes 294920 | tf_op jit(solution)/shard_map/while/body/eval_jaxpr/ppermute | solution.py:13
  1659.7 314.3 %all-reduce.5.cloned.1.call-start = ((), (), s32[]{:S(2)}) async-start(), calls=%async_computation.1 | async-start | bytes 1376256 | tf_op jit(solution)/shard_map/psum | solution.py:197
  (136 other events, 1194.4 us)
Sparse Core Ops, SparseCore 0:
  1659.8 248.4 all-reduce.2
  1910.8 27.3 all-reduce.4
